TPU v7x, 32 devices: a whole 2x2x4 slice. The times are simulated.
32 devices in a mesh: expert: 8 (over z, x), shard: 4 (over y, core).
Axes of the slice: x: 2, y: 2, z: 4, core: 2. Of those that a mesh axis runs over, the one named last changes fastest.
Arguments:
- tokens: bfloat16 [25216, 512], P(('expert', 'shard')), may hold values from -6 to 6
- teacher: bfloat16 [25216, 512], P(('expert', 'shard')), may hold values from -6 to 6
- valid_mask: int32 [25216], P(('expert', 'shard')), may hold values from 0 to 1, as said below
- routes: int32 [25216, 2], P(('expert', 'shard')), may hold values from 0 to 7, all different within a row; in each aligned block of 788 rows (0 to 787, 788 to 1575, ...) at most 394 rows name the same one
- mixer_weight: bfloat16 [512, 1536], P('shard'), may hold values from -0.25 to 0.25
- merge_weight: bfloat16 [512, 512], P('shard'), may hold values from -1 to 1
- router_weight: bfloat16 [512, 8], P('shard'), may hold values from -0.1875 to 0.1875
- norm_gain: bfloat16 [2, 512], P(None, 'shard'), may hold values from 0.5 to 1.5
- norm_shift: bfloat16 [2, 512], P(None, 'shard'), may hold values from -0.59765625 to 0.59765625
- up_weight: bfloat16 [8, 512, 2048], P('expert', None, 'shard'), may hold values from -0.25 to 0.25
- inner_bias: bfloat16 [8, 2048], P('expert', 'shard'), may hold values from -0.59765625 to 0.59765625
- down_weight: bfloat16 [8, 2048, 512], P('expert', 'shard'), may hold values from -0.75 to 0.75
- outer_bias: bfloat16 [8, 512], P('expert', 'shard'), may hold values from -6 to 6
Outputs:
- output: bfloat16 [25216, 512], P(('expert', 'shard'))
- loss_value: float32 [], replicated
- token_grad: float32 [25216, 512], P(('expert', 'shard'))
- mixer_grad: float32 [512, 1536], P('shard')
- merge_grad: float32 [512, 512], P('shard')
- router_grad: float32 [512, 8], P('shard')
- gain_grad: float32 [2, 512], P(None, 'shard')
- shift_grad: float32 [2, 512], P(None, 'shard')
- up_grad: float32 [8, 512, 2048], P('expert', None, 'shard')
- inner_grad: float32 [8, 2048], P('expert', 'shard')
- down_grad: float32 [8, 2048, 512], P('expert', 'shard')
- outer_grad: float32 [8, 512], P('expert', 'shard')
Inputs may be any that keep to these rules, and one draw needn't show every extreme that they name: `routes`: each token names two different experts. Among the 2 x 788 choices of the tokens of one device no expert is named more than 394 times, a bound that some block reaches. `valid_mask`: the first of each device's 788 tokens is valid.
All inputs are finite; a program needn't handle non-finite values.
Results may differ from a plain program's by a relative error of at most 0.011.
Values may be sent and summed in bfloat16 or wider, within the bound.
No kernel may reach another device: no remote copies, remote signals or barrier semaphores. Data moves between devices by JAX's collectives and lax.ppermute only.
A program may use at most 192 MiB of HBM per device.

v0:
```python
import jax
import jax.numpy as jnp
from jax import lax
from jax.sharding import PartitionSpec as P

HEADS = 8
HEAD_DIM = 64
SEQ = 197
norm_eps = 1e-06


def layer_norm(inputs, scale_row, shift_row):
    centered = inputs - jnp.mean(inputs, axis=-1, keepdims=True)
    variance = jnp.mean(centered * centered, axis=-1, keepdims=True)
    return centered * lax.rsqrt(variance + norm_eps) * scale_row + shift_row


def gelu_tanh(values):
    return jax.nn.gelu(values, approximate=True)


def group_sources(arrays):
    count_src = arrays.shape[0]
    group_size = 8
    return arrays.reshape((count_src // group_size, group_size) + arrays.shape[1:])


def per_device(
    tokens,
    teacher,
    valid_mask,
    routes,
    mixer_weight,
    merge_weight,
    router_weight,
    norm_gain,
    norm_shift,
    up_weight,
    inner_bias,
    down_weight,
    outer_bias,
):
    expert_ways = lax.axis_size("expert")
    shard_ways = lax.axis_size("shard")
    token_count = tokens.shape[0]
    model_width = tokens.shape[1]
    images = token_count // SEQ
    experts = router_weight.shape[1]
    local_experts = up_weight.shape[0]
    capacity = max(2, 4 * token_count // experts)
    scaling = HEAD_DIM ** (-0.5)
    (
        mixer_full,
        merge_full,
        router_full,
        gain_full,
        shift_full,
        up_full,
        inner_full,
        down_full,
        outer_full,
    ) = (
        lax.all_gather(mixer_weight, "shard", axis=0, tiled=True),
        lax.all_gather(merge_weight, "shard", axis=0, tiled=True),
        lax.all_gather(router_weight, "shard", axis=0, tiled=True),
        lax.all_gather(norm_gain, "shard", axis=1, tiled=True),
        lax.all_gather(norm_shift, "shard", axis=1, tiled=True),
        lax.all_gather(up_weight, "shard", axis=2, tiled=True),
        lax.all_gather(inner_bias, "shard", axis=1, tiled=True),
        lax.all_gather(down_weight, "shard", axis=1, tiled=True),
        lax.all_gather(outer_bias, "shard", axis=1, tiled=True),
    )
    gain_rows = gain_full.astype(jnp.float32)
    shift_rows = shift_full.astype(jnp.float32)
    inner_rows = inner_full.astype(jnp.float32)
    outer_rows = outer_full.astype(jnp.float32)
    token_rows = tokens.astype(jnp.float32)
    normed_wide, norm_one_back = jax.vjp(layer_norm, token_rows, gain_rows[0], shift_rows[0])
    normed = normed_wide.astype(jnp.bfloat16)
    mixed_rows = jnp.dot(normed, mixer_full, preferred_element_type=jnp.float32).astype(
        jnp.bfloat16
    )
    shaped = mixed_rows.reshape(images, SEQ, 3, HEADS, HEAD_DIM)
    queries = shaped[:, :, 0]
    key_rows = shaped[:, :, 1]
    value_rows = shaped[:, :, 2]
    scores = (
        jnp.einsum("bqhd,bkhd->bhqk", queries, key_rows, preferred_element_type=jnp.float32)
        * scaling
    )
    top_score = jnp.max(scores, axis=-1, keepdims=True)
    log_total = top_score + jnp.log(jnp.sum(jnp.exp(scores - top_score), axis=-1, keepdims=True))
    weights_low = jnp.exp(scores - log_total).astype(jnp.bfloat16)
    attended = jnp.einsum(
        "bhqk,bkhd->bqhd", weights_low, value_rows, preferred_element_type=jnp.float32
    )
    attended = attended.reshape(token_count, model_width).astype(jnp.bfloat16)
    residual = token_rows + jnp.dot(attended, merge_full, preferred_element_type=jnp.float32)
    normed_two_wide, norm_two_back = jax.vjp(layer_norm, residual, gain_rows[1], shift_rows[1])
    normed_two = normed_two_wide.astype(jnp.bfloat16)
    logits = jnp.dot(normed_two, router_full, preferred_element_type=jnp.float32)
    route_hot = (routes[:, :, None] == jnp.arange(experts, dtype=jnp.int32)[None, None, :]).astype(
        jnp.float32
    )

    def gate_of_logits(logit_rows):
        return jnp.sum(jax.nn.softmax(logit_rows, axis=-1)[:, None, :] * route_hot, axis=2)

    gate_values, gate_back = jax.vjp(gate_of_logits, logits)
    flat_routes = routes.reshape(-1)
    flat_hot = (flat_routes[:, None] == jnp.arange(experts, dtype=jnp.int32)[None, :]).astype(
        jnp.int32
    )
    earlier = jnp.cumsum(flat_hot, axis=0) - flat_hot
    slot_rows = flat_routes * capacity + jnp.sum(earlier * flat_hot, axis=1)
    send_rows = (
        jnp.zeros((experts * capacity, model_width), jnp.bfloat16)
        .at[slot_rows]
        .set(jnp.repeat(normed_two, 2, axis=0))
    )
    send_rows = send_rows.reshape(expert_ways, local_experts, capacity, model_width)

    def expert_rows(arrived_block):
        hidden = (
            jnp.einsum("sjcd,jdf->sjcf", arrived_block, up_full, preferred_element_type=jnp.float32)
            + inner_rows[None, :, None, :]
        )
        active = gelu_tanh(hidden).astype(jnp.bfloat16)
        produced = (
            jnp.einsum("sjcf,jfd->sjcd", active, down_full, preferred_element_type=jnp.float32)
            + outer_rows[None, :, None, :]
        )
        return produced.astype(jnp.bfloat16)

    arrived_rows = lax.all_to_all(send_rows, "expert", split_axis=0, concat_axis=0, tiled=True)
    produced = lax.map(expert_rows, group_sources(arrived_rows)).reshape(arrived_rows.shape)
    arrived, produced = (arrived_rows, produced)
    returned = lax.all_to_all(produced, "expert", split_axis=0, concat_axis=0, tiled=True)
    picked = (
        returned.reshape(experts * capacity, model_width)[slot_rows]
        .reshape(token_count, 2, model_width)
        .astype(jnp.float32)
    )
    block_out = residual + jnp.sum(gate_values[:, :, None] * picked, axis=1)
    valid_rows = valid_mask.astype(jnp.float32)
    error_rows = block_out - teacher.astype(jnp.float32)
    squared_sum = jnp.sum(valid_rows * jnp.sum(error_rows * error_rows, axis=1))
    total_error, total_count = lax.psum((squared_sum, jnp.sum(valid_rows)), ("expert", "shard"))
    loss_value = total_error / (2.0 * total_count)
    all_tokens = token_count * expert_ways * shard_ways
    final_grad = all_tokens / total_count * valid_rows[:, None] * error_rows
    gate_grad = jnp.sum(final_grad[:, None, :] * picked, axis=2)
    logit_low = gate_back(gate_grad)[0].astype(jnp.bfloat16)
    router_term = jnp.einsum("td,te->de", normed_two, logit_low, preferred_element_type=jnp.float32)
    router_back = jnp.einsum(
        "te,de->td", logit_low, router_full, preferred_element_type=jnp.float32
    )
    sent_grad = (
        (gate_values[:, :, None] * final_grad[:, None, :])
        .astype(jnp.bfloat16)
        .reshape(2 * token_count, model_width)
    )
    grad_send = (
        jnp.zeros((experts * capacity, model_width), jnp.bfloat16).at[slot_rows].set(sent_grad)
    )
    grad_send = grad_send.reshape(expert_ways, local_experts, capacity, model_width)
    grad_arrived = lax.all_to_all(grad_send, "expert", split_axis=0, concat_axis=0, tiled=True)

    def expert_backward(totals, pieces):
        up_total, inner_total, down_total, outer_total = totals
        inputs_block, grads_block = pieces
        hidden = (
            jnp.einsum("sjcd,jdf->sjcf", inputs_block, up_full, preferred_element_type=jnp.float32)
            + inner_rows[None, :, None, :]
        )
        active_wide, gelu_back = jax.vjp(gelu_tanh, hidden)
        active = active_wide.astype(jnp.bfloat16)
        down_total = down_total + jnp.einsum(
            "sjcf,sjcd->jfd", active, grads_block, preferred_element_type=jnp.float32
        )
        outer_total = outer_total + jnp.sum(grads_block.astype(jnp.float32), axis=(0, 2))
        active_grad = jnp.einsum(
            "sjcd,jfd->sjcf", grads_block, down_full, preferred_element_type=jnp.float32
        )
        hidden_grad = gelu_back(active_grad)[0].astype(jnp.bfloat16)
        inner_total = inner_total + jnp.sum(hidden_grad.astype(jnp.float32), axis=(0, 2))
        up_total = up_total + jnp.einsum(
            "sjcd,sjcf->jdf", inputs_block, hidden_grad, preferred_element_type=jnp.float32
        )
        input_grad = jnp.einsum(
            "sjcf,jdf->sjcd", hidden_grad, up_full, preferred_element_type=jnp.float32
        ).astype(jnp.bfloat16)
        return ((up_total, inner_total, down_total, outer_total), input_grad)

    expert_init = (
        jnp.zeros(up_full.shape, jnp.float32),
        jnp.zeros(inner_full.shape, jnp.float32),
        jnp.zeros(down_full.shape, jnp.float32),
        jnp.zeros(outer_full.shape, jnp.float32),
    )
    expert_totals, input_grads = lax.scan(
        expert_backward, expert_init, (group_sources(arrived), group_sources(grad_arrived))
    )
    up_total, inner_total, down_total, outer_total = expert_totals
    grad_back = lax.all_to_all(
        input_grads.reshape(arrived.shape), "expert", split_axis=0, concat_axis=0, tiled=True
    )
    moe_norm_grad = jnp.sum(
        grad_back.reshape(experts * capacity, model_width)[slot_rows]
        .reshape(token_count, 2, model_width)
        .astype(jnp.float32),
        axis=1,
    )
    norm_two_grad = moe_norm_grad + router_back
    residual_ln_grad, gain_two_grad, shift_two_grad = norm_two_back(norm_two_grad)
    residual_grad = final_grad + residual_ln_grad
    residual_low = residual_grad.astype(jnp.bfloat16)
    merge_term = jnp.einsum("tc,td->cd", attended, residual_low, preferred_element_type=jnp.float32)
    attended_grad = jnp.einsum(
        "td,cd->tc", residual_low, merge_full, preferred_element_type=jnp.float32
    ).astype(jnp.bfloat16)
    attended_grad = attended_grad.reshape(images, SEQ, HEADS, HEAD_DIM)
    again_scores = (
        jnp.einsum("bqhd,bkhd->bhqk", queries, key_rows, preferred_element_type=jnp.float32)
        * scaling
    )
    weights_wide = jnp.exp(again_scores - log_total)
    value_grad = jnp.einsum(
        "bhqk,bqhd->bkhd",
        weights_wide.astype(jnp.bfloat16),
        attended_grad,
        preferred_element_type=jnp.float32,
    )
    weight_grad = jnp.einsum(
        "bqhd,bkhd->bhqk", attended_grad, value_rows, preferred_element_type=jnp.float32
    )
    inner_dot = jnp.sum(weights_wide * weight_grad, axis=-1, keepdims=True)
    score_grad = (weights_wide * (weight_grad - inner_dot)).astype(jnp.bfloat16)
    query_grad = (
        jnp.einsum("bhqk,bkhd->bqhd", score_grad, key_rows, preferred_element_type=jnp.float32)
        * scaling
    )
    key_grad = (
        jnp.einsum("bhqk,bqhd->bkhd", score_grad, queries, preferred_element_type=jnp.float32)
        * scaling
    )
    mixed_grad = (
        jnp.stack([query_grad, key_grad, value_grad], axis=2)
        .reshape(token_count, 3 * model_width)
        .astype(jnp.bfloat16)
    )
    mixer_term = jnp.einsum("tc,tm->cm", normed, mixed_grad, preferred_element_type=jnp.float32)
    norm_one_grad = jnp.einsum(
        "tm,cm->tc", mixed_grad, mixer_full, preferred_element_type=jnp.float32
    )
    token_ln_grad, gain_one_grad, shift_one_grad = norm_one_back(norm_one_grad)
    token_grad = residual_grad + token_ln_grad
    gain_term = jnp.stack([gain_one_grad, gain_two_grad], axis=0)
    shift_term = jnp.stack([shift_one_grad, shift_two_grad], axis=0)
    summed = lax.psum(
        (mixer_term, merge_term, router_term, gain_term, shift_term), ("expert", "shard")
    )
    position = lax.axis_index("shard")
    rows_dev = model_width // shard_ways
    mixer_grad = lax.dynamic_slice_in_dim(summed[0], position * rows_dev, rows_dev, 0)
    merge_grad = lax.dynamic_slice_in_dim(summed[1], position * rows_dev, rows_dev, 0)
    router_grad = lax.dynamic_slice_in_dim(summed[2], position * rows_dev, rows_dev, 0)
    gain_grad = lax.dynamic_slice_in_dim(summed[3], position * rows_dev, rows_dev, 1)
    shift_grad = lax.dynamic_slice_in_dim(summed[4], position * rows_dev, rows_dev, 1)
    up_grad, inner_grad, down_grad, outer_grad = (
        lax.psum_scatter(
            up_total.astype(jnp.bfloat16), "shard", scatter_dimension=2, tiled=True
        ).astype(jnp.float32),
        lax.psum_scatter(
            inner_total.astype(jnp.bfloat16), "shard", scatter_dimension=1, tiled=True
        ).astype(jnp.float32),
        lax.psum_scatter(
            down_total.astype(jnp.bfloat16), "shard", scatter_dimension=1, tiled=True
        ).astype(jnp.float32),
        lax.psum_scatter(
            outer_total.astype(jnp.bfloat16), "shard", scatter_dimension=1, tiled=True
        ).astype(jnp.float32),
    )
    return (
        block_out.astype(jnp.bfloat16),
        loss_value,
        token_grad,
        mixer_grad,
        merge_grad,
        router_grad,
        gain_grad,
        shift_grad,
        up_grad,
        inner_grad,
        down_grad,
        outer_grad,
    )


def solution(mesh):
    in_specs = (
        P(("expert", "shard"), None),
        P(("expert", "shard"), None),
        P(("expert", "shard")),
        P(("expert", "shard"), None),
        P("shard", None),
        P("shard", None),
        P("shard", None),
        P(None, "shard"),
        P(None, "shard"),
        P("expert", None, "shard"),
        P("expert", "shard"),
        P("expert", "shard", None),
        P("expert", "shard"),
    )
    out_specs = (
        P(("expert", "shard"), None),
        P(),
        P(("expert", "shard"), None),
        P("shard", None),
        P("shard", None),
        P("shard", None),
        P(None, "shard"),
        P(None, "shard"),
        P("expert", None, "shard"),
        P("expert", "shard"),
        P("expert", "shard", None),
        P("expert", "shard"),
    )
    return jax.shard_map(
        per_device, mesh=mesh, in_specs=in_specs, out_specs=out_specs, check_vma=False
    )
```

profile of v0, /device:TPU:0, one launch (start us, length us, event | category | flops | bytes accessed | tf_op | source)
XLA Modules:
  0.0 810.7 jit_solution(4811789456164737185)
XLA Ops:
  13.1 6.2 all_gather.27
  25.4 9.2 %all_gather.30 = bf16[512,512]{1,0:T(8,128)(2,1)} all-gather(bf16[128,512]{1,0:T(8,128)(2,1)S(1)} %copy-done.31), channel_id=1, replica_groups=mesh['expert'=8,'shard'=4] {'shard'}, dimensions={0}, use_global_device_ids=true | all-gather | bytes 655360 | tf_op jit(solution)/shard_map/all_gather | solution.py:64
  68.2 13.4 %scatter_custom_fusion = bf16[3152,512]{1,0:T(8,128)(2,1)} fusion(s32[1576]{0:T(1024)S(1)} %fusion.91, bf16[1576,512]{1,0:T(8,128)(2,1)} %reshape.306, bf16[]{:T(256)} %constant.84.clone.1), kind=kCustom, calls=%fused_computation.86 | custom fusion | bytes 3228160 | tf_op jit(solution)/shard_map/scatter | solution.py:119
  102.6 13.8 %all-gather.6.cloned.1.call-done = bf16[1,512,2048]{2,1,0:T(8,128)(2,1)} async-done(((bf16[1,512,512]{2,1,0:T(8,128)(2,1)}), bf16[1,512,2048]{2,1,0:T(8,128)(2,1)}) %all-gather.6.cloned.1.call-update) | async-done | bytes 2097168 | tf_op jit(solution)/shard_map/all_gather | solution.py:68
  116.3 48.6 %all-to-all-done = bf16[8,1,394,512]{3,2,1,0:T(8,128)(2,1)} async-done(((bf16[8,1,394,512]{3,2,1,0:T(8,128)(2,1)}), bf16[8,1,394,512]{3,2,1,0:T(8,128)(2,1)}, u32[]{:S(2)}, u32[]{:S(2)}) %all-to-all-start) | async-done | bytes 3227680 | tf_op jit(solution)/shard_map/all_to_all | solution.py:135
  165.0 14.3 %fusion.25 = f32[8,394,2048]{2,1,0:T(8,128)} fusion(bf16[8,1,394,512]{3,2,1,0:T(8,128)(2,1)} %all-to-all-done, bf16[1,512,2048]{2,1,0:T(8,128)(2,1)} %all-gather.6.cloned.1.call-done), kind=kOutput, calls=%fused_computation.44 | convolution fusion | flops 6610223104 | bytes 31145984 | tf_op jit(solution)/shard_map/while/body/eval_jaxpr/sjcd,jdf->sjcf/dot_general | solution.py:125
  179.3 17.0 %fusion.21 = bf16[8,1,394,512]{3,2,1,0:T(8,128)(2,1)} fusion(f32[512]{0:T(512)S(1)} %bitcast.253, bf16[1,2048,512]{2,1,0:T(8,128)(2,1)} %all-gather.8.cloned.1.call-done, f32[8,394,2048]{2,1,0:T(8,128)} %fusion.25, f32[2048]{0:T(1024)S(1)} %bitcast.250), kind=kOutput, calls=%fused_computation.40 | convolution fusion | flops 6678003712 | bytes 31156224 | tf_op jit(solution)/shard_map/while/body/eval_jaxpr/sjcf,jfd->sjcd/dot_general | solution.py:130
  201.5 92.6 %psum.50 = f32[]{:T(128)} all-reduce(f32[]{:T(128)} %convert_reduce_fusion.1), channel_id=1, replica_groups=mesh['expert'=8,'shard'=4] {'expert','shard'}, use_global_device_ids=true, to_apply=%region_18.19 | all-reduce | flops 1 | bytes 8 | tf_op jit(solution)/shard_map/psum | solution.py:148
  304.4 6.0 gather_fusion
  314.1 17.6 %multiply_reduce_fusion.3 = f32[788,512]{1,0:T(8,128)S(1)} fusion(f32[788,2,512]{2,1,0:T(2,128)S(1)} %reshape.284, f32[788,2]{1,0:T(8,128)} %copy-done.27), kind=kLoop, calls=%fused_computation.49 | loop fusion | flops 1210368 | bytes 4847776 | tf_op jit(solution)/shard_map/reduce_sum | solution.py:144
  342.1 18.5 %scatter_custom_fusion.1 = bf16[3152,512]{1,0:T(8,128)(2,1)} fusion(s32[1576]{0:T(1024)S(1)} %fusion.91, f32[1576,512]{1,0:T(8,128)} %mul.344, f32[1576]{0:T(1024)S(1)} %mul.341, bf16[]{:T(256)} %constant.84.clone.1), kind=kCustom, calls=%fused_computation.83 | custom fusion | flops 1613824 | bytes 6463490 | tf_op jit(solution)/shard_map/scatter | solution.py:164
  364.2 79.0 %all_to_all.20 = bf16[8,1,394,512]{3,2,1,0:T(8,128)(2,1)} all-to-all(bf16[8,1,394,512]{3,2,1,0:T(8,128)(2,1)} %bitcast.233), channel_id=1, replica_groups=mesh['expert'=8,'shard'=4] {'expert'}, dimensions={0} | all-to-all | bytes 6455296 | tf_op jit(solution)/shard_map/all_to_all | solution.py:167
  446.5 30.0 %fusion.115 = (bf16[2048]{0:T(1024)(128)(2,1)S(1)}, bf16[8,1,394,2048]{3,2,0,1:T(8,128)(2,1)}) fusion(f32[2048]{0:T(1024)S(1)} %bitcast.251, f32[8,394,2048]{2,1,0:T(8,128)} %fusion.25, bf16[1,2048,512]{2,1,0:T(8,128)(2,1)} %all-gather.8.cloned.1.call-done, bf16[8,1,394,512]{3,2,1,0:T(8,128)(2,1)} %all_to_all.20), kind=kOutput, calls=%fused_computation.173 | convolution fusion | flops 6752237568 | bytes 44068864 | tf_op jit(solution)/shard_map/while/body/eval_jaxpr/sjcd,jfd->sjcf/dot_general | solution.py:182
  477.7 18.2 %fusion.42 = bf16[1,2048,512]{2,1,0:T(8,128)(2,1)} fusion(bf16[8,1,394,512]{3,2,1,0:T(8,128)(2,1)} %all_to_all.20, f32[8,394,2048]{2,1,0:T(8,128)} %fusion.25, f32[2048]{0:T(1024)S(1)} %bitcast.252), kind=kOutput, calls=%fused_computation.52 | convolution fusion | flops 6675824640 | bytes 31154176 | tf_op jit(solution)/shard_map/while/body/eval_jaxpr/sjcf,sjcd->jfd/dot_general | solution.py:178
  496.0 13.6 %convert_bitcast_fusion = bf16[8,1,394,512]{3,2,1,0:T(8,128)(2,1)} fusion(bf16[8,1,394,2048]{3,2,0,1:T(8,128)(2,1)} %get-tuple-element.101, bf16[1,512,2048]{2,1,0:T(8,128)(2,1)} %all-gather.6.cloned.1.call-done), kind=kOutput, calls=%fused_computation.46 | convolution fusion | flops 6611836928 | bytes 18235392 | tf_op jit(solution)/shard_map/while/body/eval_jaxpr/sjcf,jdf->sjcd/dot_general | solution.py:190
  514.1 12.2 %fusion.37 = bf16[1,512,2048]{2,1,0:T(8,128)(2,1)} fusion(bf16[8,1,394,2048]{3,2,0,1:T(8,128)(2,1)} %get-tuple-element.101, bf16[8,1,394,512]{3,2,1,0:T(8,128)(2,1)} %all-to-all-done), kind=kOutput, calls=%fused_computation.51 | convolution fusion | flops 6611271680 | bytes 18235392 | tf_op jit(solution)/shard_map/while/body/eval_jaxpr/sjcd,sjcf->jdf/dot_general | solution.py:187
  538.9 27.8 %reduce-scatter.9.cloned.1.call-done = bf16[1,512,512]{2,1,0:T(8,128)(2,1)} async-done(((bf16[1,512,2048]{2,1,0:T(8,128)(2,1)}), bf16[1,512,512]{2,1,0:T(8,128)(2,1)}) %reduce-scatter.9.cloned.1.call-update) | async-done | bytes 524304 | tf_op jit(solution)/shard_map/reduce_scatter | solution.py:271
  568.8 18.0 %all-to-all-done.3 = bf16[8,1,394,512]{3,2,1,0:T(8,128)(2,1)} async-done(((bf16[8,1,394,512]{3,2,1,0:T(8,128)(2,1)}), bf16[8,1,394,512]{3,2,1,0:T(8,128)(2,1)}, u32[]{:S(2)}, u32[]{:S(2)}) %all-to-all-start.3) | async-done | bytes 3227680 | tf_op jit(solution)/shard_map/all_to_all | solution.py:205
  589.2 6.0 gather_fusion.1
  600.2 7.1 reduce_sum.310
  619.7 7.8 multiply_reduce_fusion
  643.1 7.0 convert_element_type.174
  663.1 39.3 %all-reduce.1 = (f32[]{:T(128)}, f32[512,8]{0,1:T(8,128)S(1)}, f32[2,512]{1,0:T(2,128)S(1)}, f32[2,512]{1,0:T(2,128)S(1)}) all-reduce(f32[]{:T(128)} %get-tuple-element.103, f32[512,8]{0,1:T(8,128)S(1)} %fusion.116, f32[2,512]{1,0:T(2,128)S(1)} %pad_maximum_fusion.1, ...), channel_id=1, replica_groups=mesh['expert'=8,'shard'=4] {'expert','shard'}, use_global_device_ids=true, to_apply=%region_16.17 | all-reduce | flops 6145 | bytes 49160 | tf_op jit(solution)/shard_map/psum | solution.py:148
  708.0 90.6 %all-reduce.5.cloned.1.call-done = (f32[512,1536]{1,0:T(8,128)}, f32[512,512]{1,0:T(8,128)}) async-done(((f32[512,1536]{1,0:T(8,128)}, f32[512,512]{1,0:T(8,128)}), (f32[512,1536]{1,0:T(8,128)}, f32[512,512]{1,0:T(8,128)})) %all-reduce.5.cloned.1.call-update) | async-done | bytes 4194320 | tf_op jit(solution)/shard_map/psum | solution.py:260
  (251 shorter events, 178.1 us)
Async XLA Ops:
  7.2 17.6 %copy-start.9 = (bf16[788,512]{1,0:T(8,128)(2,1)S(1)}, bf16[788,512]{1,0:T(8,128)(2,1)}, u32[]{:S(2)}) copy-start(bf16[788,512]{1,0:T(8,128)(2,1)} %param.13) | copy-start | bytes 2420740
  7.2 18.2 %copy-start.31 = (bf16[128,512]{1,0:T(8,128)(2,1)S(1)}, bf16[128,512]{1,0:T(8,128)(2,1)}, u32[]{:S(2)}) copy-start(bf16[128,512]{1,0:T(8,128)(2,1)} %param.18) | copy-start | bytes 393220
  7.2 27.5 %all-gather.4.cloned.1.call-start = ((), (), s32[]{:S(2)}) async-start(), calls=%async_computation.8 | async-start | bytes 1966080 | tf_op jit(solution)/shard_map/all_gather | solution.py:63
  25.0 12.7 %copy-start.35 = (f32[788]{0:T(1024)}, f32[788]{0:T(1024)S(1)}, u32[]{:S(2)}) copy-start(f32[788]{0:T(1024)S(1)} %broadcast_multiply_fusion.2) | copy-start | bytes 9460
  25.4 9.3 %copy-start.39 = (f32[788]{0:T(1024)}, f32[788]{0:T(1024)S(1)}, u32[]{:S(2)}) copy-start(f32[788]{0:T(1024)S(1)} %fusion.62) | copy-start | bytes 9460
  34.6 30.6 %copy-start.46 = (f32[1,512]{1,0:T(1,128)}, f32[1,512]{1,0:T(1,128)S(1)}, u32[]{:S(2)}) copy-start(f32[1,512]{1,0:T(1,128)S(1)} %get-tuple-element.86) | copy-start | bytes 6148
  65.6 234.9 %copy-start.13 = (bf16[788,512]{1,0:T(8,128)(2,1)}, bf16[788,512]{1,0:T(8,128)(2,1)S(1)}, u32[]{:S(2)}) copy-start(bf16[788,512]{1,0:T(8,128)(2,1)S(1)} %add_convert_fusion) | copy-start | bytes 2420740
  85.2 12.3 %copy-start.54 = (bf16[1,128]{1,0:T(2,128)(2,1)S(1)}, bf16[1,128]{1,0:T(2,128)(2,1)}, u32[]{:S(2)}) copy-start(bf16[1,128]{1,0:T(2,128)(2,1)} %param.25) | copy-start | bytes 772
  85.2 79.8 %all-to-all-start = ((bf16[8,1,394,512]{3,2,1,0:T(8,128)(2,1)}), bf16[8,1,394,512]{3,2,1,0:T(8,128)(2,1)}, u32[]{:S(2)}, u32[]{:S(2)}) async-start(bf16[8,1,394,512]{3,2,1,0:T(8,128)(2,1)} %bitcast.10), calls=%async_computation | async-start | bytes 6553600 | tf_op jit(solution)/shard_map/all_to_all | solution.py:135
  90.8 25.5 %all-gather.6.cloned.1.call-start = ((), (), s32[]{:S(2)}) async-start(), calls=%async_computation.9 | async-start | bytes 2621440 | tf_op jit(solution)/shard_map/all_gather | solution.py:68
  91.6 87.7 %all-gather.8.cloned.1.call-start = ((), (), s32[]{:S(2)}) async-start(), calls=%async_computation.10 | async-start | bytes 2621440 | tf_op jit(solution)/shard_map/all_gather | solution.py:70
  196.2 98.6 %copy-start.51 = (bf16[128,8]{0,1:T(8,128)(2,1)S(1)}, bf16[128,8]{0,1:T(8,128)(2,1)}, u32[]{:S(2)}) copy-start(bf16[128,8]{0,1:T(8,128)(2,1)} %param.19) | copy-start | bytes 6148
  196.2 104.6 %copy-start.32 = (s32[788,2]{0,1:T(2,128)S(1)}, s32[788,2]{0,1:T(2,128)}, u32[]{:S(2)}) copy-start(s32[788,2]{0,1:T(2,128)} %param.16) | copy-start | bytes 18916
  196.2 105.6 %all-to-all-start.1 = ((bf16[8,1,394,512]{3,2,1,0:T(8,128)(2,1)}), bf16[8,1,394,512]{3,2,1,0:T(8,128)(2,1)}, u32[]{:S(2)}, u32[]{:S(2)}) async-start(bf16[8,1,394,512]{3,2,1,0:T(8,128)(2,1)} %fusion.21), calls=%async_computation.1 | async-start | bytes 6553600 | tf_op jit(solution)/shard_map/all_to_all | solution.py:138
  200.9 332.9 %reduce-scatter.15.cloned.1.call-start = ((), (), s32[]{:S(2)}) async-start(), calls=%async_computation.14 | async-start | bytes 163840
  314.1 17.7 %copy-start.2 = (f32[788,512]{1,0:T(8,128)S(1)}, f32[788,512]{1,0:T(8,128)}, u32[]{:S(2)}) copy-start(f32[788,512]{1,0:T(8,128)} %copy-done.1) | copy-start | bytes 4841476
  314.1 17.7 %copy-start.28 = (bf16[788,512]{1,0:T(8,128)(2,1)S(1)}, bf16[788,512]{1,0:T(8,128)(2,1)}, u32[]{:S(2)}) copy-start(bf16[788,512]{1,0:T(8,128)(2,1)} %param.14) | copy-start | bytes 2420740
  446.4 88.7 %reduce-scatter.13.cloned.1.call-start = ((), (), s32[]{:S(2)}) async-start(), calls=%async_computation.13 | async-start | bytes 655360
  477.7 59.1 %reduce-scatter.11.cloned.1.call-start = ((), (), s32[]{:S(2)}) async-start(), calls=%async_computation.12 | async-start | bytes 2621440 | tf_op jit(solution)/shard_map/reduce_scatter | solution.py:277
  509.6 77.3 %all-to-all-start.3 = ((bf16[8,1,394,512]{3,2,1,0:T(8,128)(2,1)}), bf16[8,1,394,512]{3,2,1,0:T(8,128)(2,1)}, u32[]{:S(2)}, u32[]{:S(2)}) async-start(bf16[8,1,394,512]{3,2,1,0:T(8,128)(2,1)} %convert_bitcast_fusion), calls=%async_computation.3 | async-start | bytes 6553600 | tf_op jit(solution)/shard_map/all_to_all | solution.py:205
  514.0 52.6 %reduce-scatter.9.cloned.1.call-start = ((), (), s32[]{:S(2)}) async-start(), calls=%async_computation.11 | async-start | bytes 2621440 | tf_op jit(solution)/shard_map/reduce_scatter | solution.py:271
  526.3 272.2 %all-reduce.5.cloned.1.call-start = ((), (), s32[]{:S(2)}) async-start(), calls=%async_computation.15 | async-start | bytes 8388608 | tf_op jit(solution)/shard_map/psum | solution.py:260
  616.5 11.0 %slice-start = ((s8[6553600]{0:T(1024)(128)(4,1)}), s8[2359296]{0:T(1024)(128)(4,1)S(1)}, s32[]{:S(2)}) async-start(s8[6553600]{0:T(1024)(128)(4,1)} %bitcast.231), calls=%async_computation.16 | async-start | bytes 4718592
  661.1 43.8 %copy-start.8 = (f32[788,512]{1,0:T(8,128)S(1)}, f32[788,512]{1,0:T(8,128)}, u32[]{:S(2)}) copy-start(f32[788,512]{1,0:T(8,128)} %copy-done.6) | copy-start | bytes 4841476
  (45 other events, 165.9 us)
Sparse Core Ops, SparseCore 0:
  9.6 23.7 all-gather.3
  93.2 23.0 all-gather.5
  117.9 22.5 all-gather.7
  446.6 18.7 reduce-scatter.14
  477.8 20.7 reduce-scatter.12
  501.0 31.4 reduce-scatter.10
  535.2 31.4 reduce-scatter.8
  656.1 142.4 all-reduce.4
where the time goes:
time: 818 us; the launch traced here: 811 us
  blocking collectives  248 us (30%)
  waiting for transfers between devices  201 us (25%)
  matrix products  143 us (17%)
  local copies, waits for them, and re-layouts  113 us (14%)
  other arithmetic  72.9 us (9%)
  between operations  18.7 us (2%)
  starting transfers between devices  15.2 us (2%)
    psum x2, blocking collectives, per_device(): lax.psum((squared_sum, jnp.sum(valid_rows)), ('expert', 'shard'))  132 us
    psum x1, waiting for transfers between devices, per_device(): lax.psum((mixer_term, merge_term, router_term, gain_term, shift_term), ('...  90.6 us
    all_to_all x1, blocking collectives, per_device(): lax.all_to_all(grad_send, 'expert', split_axis=0, concat_axis=0, tiled=True)  79 us
    all_to_all x1, waiting for transfers between devices, per_device(): lax.all_to_all(send_rows, 'expert', split_axis=0, concat_axis=0, tiled=True)  48.6 us
    dot_general x1, matrix products, expert_backward(): jnp.einsum('sjcd,jfd->sjcf', grads_block, down_full, preferred_element_ty...  30 us
    reduce_scatter x1, waiting for transfers between devices, per_device(): lax.psum_scatter(up_total.astype(jnp.bfloat16), 'shard', scatter_dimensio...  27.8 us
    unnamed x125, local copies, waits for them, and re-layouts  19.9 us
    scatter x1, other arithmetic, per_device(): jnp.zeros((experts * capacity, model_width), jnp.bfloat16).at[slot_rows]  18.5 us
  transfers between devices with their start and end apart: 11, of which 5 were waited for; matrix products, arithmetic and copies ran while one was open for 15% of the time, Pallas kernels for 0%

commit v1 on v0

--- a/solution.py
+++ b/solution.py
@@ -145,7 +145,9 @@
     valid_rows = valid_mask.astype(jnp.float32)
     error_rows = block_out - teacher.astype(jnp.float32)
     squared_sum = jnp.sum(valid_rows * jnp.sum(error_rows * error_rows, axis=1))
-    total_error, total_count = lax.psum((squared_sum, jnp.sum(valid_rows)), ("expert", "shard"))
+    total_error, total_count = lax.psum(
+        lax.psum((squared_sum, jnp.sum(valid_rows)), "shard"), "expert"
+    )
     loss_value = total_error / (2.0 * total_count)
     all_tokens = token_count * expert_ways * shard_ways
     final_grad = all_tokens / total_count * valid_rows[:, None] * error_rows

time: 818 us -> 775 us (0.947)
  waiting for transfers between devices: 201 us -> 151 us
  blocking collectives: 248 us -> 260 us
  matrix products: 143 us -> 133 us
    psum x1, waiting for transfers between devices: 90.6 us -> 59.8 us  [per_device(): lax.psum((mixer_term, merge_term, router_term, gain_term, shift_term), ('...]
    reduce_scatter x1, waiting for transfers between devices: 27.8 us -> 0.01 us  [per_device(): lax.psum_scatter(up_total.astype(jnp.bfloat16), 'shard', scatter_dimensio...]
    all_to_all x1, blocking collectives: 79 us -> 91 us  [per_device(): lax.all_to_all(grad_send, 'expert', split_axis=0, concat_axis=0, tiled=True)]
    unnamed x125 -> x133, local copies, waits for them, and re-layouts: 19.9 us -> 24.8 us
    psum x2 -> x5, blocking collectives: 132 us -> 133 us  [the longest x2 82.1 us: per_device(): lax.psum(lax.psum((squared_sum, jnp.sum(valid_rows)), 'shard'), 'expert')]
  transfers between devices with their start and end apart: 11 -> 11, of which waited for: 5 -> 5; matrix products, arithmetic and copies ran while one was open for 15% -> 19% of each run, Pallas kernels for 0% -> 0%
where the time goes in v1:
time: 775 us; the launch traced here: 768 us
  blocking collectives  260 us (34%)
  waiting for transfers between devices  151 us (19%)
  matrix products  133 us (17%)
  local copies, waits for them, and re-layouts  117 us (15%)
  other arithmetic  72.9 us (9%)
  between operations  18.5 us (2%)
  starting transfers between devices  15.7 us (2%)
    all_to_all x1, blocking collectives, per_device(): lax.all_to_all(grad_send, 'expert', split_axis=0, concat_axis=0, tiled=True)  91 us
    psum x2, blocking collectives, per_device(): lax.psum(lax.psum((squared_sum, jnp.sum(valid_rows)), 'shard'), 'expert')  82.1 us
    psum x1, waiting for transfers between devices, per_device(): lax.psum((mixer_term, merge_term, router_term, gain_term, shift_term), ('...  59.8 us
    all_to_all x1, waiting for transfers between devices, per_device(): lax.all_to_all(send_rows, 'expert', split_axis=0, concat_axis=0, tiled=True)  48.6 us
    psum x1, blocking collectives, per_device(): lax.psum((mixer_term, merge_term, router_term, gain_term, shift_term), ('...  37.3 us
    dot_general x1, matrix products, expert_backward(): jnp.einsum('sjcd,jfd->sjcf', grads_block, down_full, preferred_element_ty...  25.6 us
    unnamed x133, local copies, waits for them, and re-layouts  24.8 us
    all_to_all x1, waiting for transfers between devices, per_device(): lax.all_to_all(input_grads.reshape(arrived.shape), 'expert', split_axis=0...  22.8 us
  transfers between devices with their start and end apart: 11, of which 5 were waited for; matrix products, arithmetic and copies ran while one was open for 19% of the time, Pallas kernels for 0%

profile of v1, /device:TPU:0, one launch (start us, length us, event | category | flops | bytes accessed | tf_op | source)
XLA Modules:
  0.0 767.7 jit_solution(7873603987749610147)
XLA Ops:
  13.1 6.2 all_gather.27
  25.4 9.2 %all_gather.30 = bf16[512,512]{1,0:T(8,128)(2,1)} all-gather(bf16[128,512]{1,0:T(8,128)(2,1)S(1)} %copy-done.32), channel_id=1, replica_groups=mesh['expert'=8,'shard'=4] {'shard'}, dimensions={0}, use_global_device_ids=true | all-gather | bytes 655360 | tf_op jit(solution)/shard_map/all_gather | solution.py:64
  68.2 13.2 %scatter_custom_fusion = bf16[3152,512]{1,0:T(8,128)(2,1)} fusion(s32[1576]{0:T(1024)S(1)} %fusion.91, bf16[1576,512]{1,0:T(8,128)(2,1)} %reshape.306, bf16[]{:T(256)} %constant.84.clone.1), kind=kCustom, calls=%fused_computation.86 | custom fusion | bytes 3228160 | tf_op jit(solution)/shard_map/scatter | solution.py:119
  102.4 13.8 %all-gather.6.cloned.1.call-done = bf16[1,512,2048]{2,1,0:T(8,128)(2,1)} async-done(((bf16[1,512,512]{2,1,0:T(8,128)(2,1)}), bf16[1,512,2048]{2,1,0:T(8,128)(2,1)}) %all-gather.6.cloned.1.call-update) | async-done | bytes 2097168 | tf_op jit(solution)/shard_map/all_gather | solution.py:68
  116.2 48.6 %all-to-all-done = bf16[8,1,394,512]{3,2,1,0:T(8,128)(2,1)} async-done(((bf16[8,1,394,512]{3,2,1,0:T(8,128)(2,1)}), bf16[8,1,394,512]{3,2,1,0:T(8,128)(2,1)}, u32[]{:S(2)}, u32[]{:S(2)}) %all-to-all-start) | async-done | bytes 3227680 | tf_op jit(solution)/shard_map/all_to_all | solution.py:135
  164.8 14.3 %fusion.25 = f32[8,394,2048]{2,1,0:T(8,128)} fusion(bf16[8,1,394,512]{3,2,1,0:T(8,128)(2,1)} %all-to-all-done, bf16[1,512,2048]{2,1,0:T(8,128)(2,1)} %all-gather.6.cloned.1.call-done), kind=kOutput, calls=%fused_computation.44 | convolution fusion | flops 6610223104 | bytes 31145984 | tf_op jit(solution)/shard_map/while/body/eval_jaxpr/sjcd,jdf->sjcf/dot_general | solution.py:125
  179.1 16.9 %fusion.21 = bf16[8,1,394,512]{3,2,1,0:T(8,128)(2,1)} fusion(f32[512]{0:T(512)S(1)} %bitcast.253, bf16[1,2048,512]{2,1,0:T(8,128)(2,1)} %all-gather.8.cloned.1.call-done, f32[8,394,2048]{2,1,0:T(8,128)} %fusion.25, f32[2048]{0:T(1024)S(1)} %bitcast.250), kind=kOutput, calls=%fused_computation.40 | convolution fusion | flops 6678003712 | bytes 31156224 | tf_op jit(solution)/shard_map/while/body/eval_jaxpr/sjcf,jfd->sjcd/dot_general | solution.py:130
  201.3 6.7 psum.65
  208.0 61.8 %psum.66 = f32[]{:T(128)} all-reduce(f32[]{:T(128)} %psum.65), channel_id=1, replica_groups=mesh['expert'=8,'shard'=4] {'expert'}, use_global_device_ids=true, to_apply=%region_20.21 | all-reduce | flops 1 | bytes 8 | tf_op jit(solution)/shard_map/psum | solution.py:148
  289.5 17.6 %multiply_reduce_fusion.3 = f32[788,512]{1,0:T(8,128)S(1)} fusion(f32[788,2,512]{2,1,0:T(2,128)S(1)} %reshape.284, f32[788,2]{1,0:T(8,128)} %copy-done.27), kind=kLoop, calls=%fused_computation.49 | loop fusion | flops 1210368 | bytes 4847776 | tf_op jit(solution)/shard_map/reduce_sum | solution.py:144
  317.6 18.4 %scatter_custom_fusion.1 = bf16[3152,512]{1,0:T(8,128)(2,1)} fusion(s32[1576]{0:T(1024)S(1)} %fusion.91, f32[1576,512]{1,0:T(8,128)} %mul.344, f32[1576]{0:T(1024)S(1)} %mul.341, bf16[]{:T(256)} %constant.84.clone.1), kind=kCustom, calls=%fused_computation.83 | custom fusion | flops 1613824 | bytes 6463490 | tf_op jit(solution)/shard_map/scatter | solution.py:166
  339.6 91.0 %all_to_all.20 = bf16[8,1,394,512]{3,2,1,0:T(8,128)(2,1)S(1)} all-to-all(bf16[8,1,394,512]{3,2,1,0:T(8,128)(2,1)} %bitcast.233), channel_id=1, replica_groups=mesh['expert'=8,'shard'=4] {'expert'}, dimensions={0} | all-to-all | bytes 6455296 | tf_op jit(solution)/shard_map/all_to_all | solution.py:169
  430.6 25.6 %fusion.115 = (bf16[2048]{0:T(1024)(128)(2,1)S(1)}, bf16[8,1,394,2048]{3,2,0,1:T(8,128)(2,1)S(1)}) fusion(f32[2048]{0:T(1024)S(1)} %bitcast.251, f32[8,394,2048]{2,1,0:T(8,128)} %fusion.25, bf16[1,2048,512]{2,1,0:T(8,128)(2,1)S(1)} %copy-done.58, bf16[8,1,394,512]{3,2,1,0:T(8,128)(2,1)S(1)} %all_to_all.20), kind=kOutput, calls=%fused_computation.173 | convolution fusion | flops 6752237568 | bytes 44068864 | tf_op jit(solution)/shard_map/while/body/eval_jaxpr/sjcd,jfd->sjcf/dot_general | solution.py:184
  461.0 8.8 %convert_bitcast_fusion = bf16[8,1,394,512]{3,2,1,0:T(8,128)(2,1)} fusion(bf16[8,1,394,2048]{3,2,0,1:T(8,128)(2,1)S(1)} %get-tuple-element.100, bf16[1,512,2048]{2,1,0:T(8,128)(2,1)S(1)} %copy-done.57), kind=kOutput, calls=%fused_computation.46 | convolution fusion | flops 6611836928 | bytes 18235392 | tf_op jit(solution)/shard_map/while/body/eval_jaxpr/sjcf,jdf->sjcd/dot_general | solution.py:192
  479.0 18.3 %fusion.42 = bf16[1,2048,512]{2,1,0:T(8,128)(2,1)} fusion(bf16[8,1,394,512]{3,2,1,0:T(8,128)(2,1)} %copy-done.12, f32[8,394,2048]{2,1,0:T(8,128)} %fusion.25, f32[2048]{0:T(1024)S(1)} %bitcast.252), kind=kOutput, calls=%fused_computation.52 | convolution fusion | flops 6675824640 | bytes 31154176 | tf_op jit(solution)/shard_map/while/body/eval_jaxpr/sjcf,sjcd->jfd/dot_general | solution.py:180
  504.6 12.4 %fusion.37 = bf16[1,512,2048]{2,1,0:T(8,128)(2,1)} fusion(bf16[8,1,394,2048]{3,2,0,1:T(8,128)(2,1)} %copy-done.59, bf16[8,1,394,512]{3,2,1,0:T(8,128)(2,1)} %all-to-all-done), kind=kOutput, calls=%fused_computation.51 | convolution fusion | flops 6611271680 | bytes 18235392 | tf_op jit(solution)/shard_map/while/body/eval_jaxpr/sjcd,sjcf->jdf/dot_general | solution.py:189
  524.2 22.8 %all-to-all-done.3 = bf16[8,1,394,512]{3,2,1,0:T(8,128)(2,1)} async-done(((bf16[8,1,394,512]{3,2,1,0:T(8,128)(2,1)}), bf16[8,1,394,512]{3,2,1,0:T(8,128)(2,1)}, u32[]{:S(2)}, u32[]{:S(2)}) %all-to-all-start.3) | async-done | bytes 3227680 | tf_op jit(solution)/shard_map/all_to_all | solution.py:207
  560.4 7.1 reduce_sum.310
  580.0 7.8 %multiply_reduce_fusion = (f32[4,8,197]{2,1,0:T(8,128)S(1)}, f32[4,8,197,197]{2,3,1,0:T(8,128)}) fusion(f32[4,8,197,197]{2,3,1,0:T(8,128)} %copy-done, f32[4,8,197]{2,1,0:T(8,128)S(1)} %copy-done.31, bf16[4,197,8,64]{1,3,2,0:T(8,128)(2,1)} %copy.115, bf16[4,197,1,8,64]{1,4,3,0,2:T(8,128)(2,1)S(1)} %copy-done.19), kind=kOutput, calls=%fused_computation.32 | convolution fusion | flops 163922912 | bytes 11599360 | tf_op jit(solution)/shard_map/bqhd,bkhd->bhqk/dot_general | solution.py:236
  601.3 7.1 convert_element_type.174
  618.2 6.7 psum.63
  627.1 20.3 %psum.64 = f32[]{:T(128)} all-reduce(f32[]{:T(128)} %psum.63), channel_id=1, replica_groups=mesh['expert'=8,'shard'=4] {'expert'}, use_global_device_ids=true, to_apply=%region_17.18 | all-reduce | flops 1 | bytes 8 | tf_op jit(solution)/shard_map/psum | solution.py:148
  654.3 37.3 %all-reduce.1 = (f32[512,8]{0,1:T(8,128)S(1)}, f32[2,512]{1,0:T(2,128)S(1)}, f32[2,512]{1,0:T(2,128)S(1)}) all-reduce(f32[512,8]{0,1:T(8,128)S(1)} %fusion.116, f32[2,512]{1,0:T(2,128)S(1)} %pad_maximum_fusion.1, f32[2,512]{1,0:T(2,128)S(1)} %pad_maximum_fusion.2), channel_id=1, replica_groups=mesh['expert'=8,'shard'=4] {'expert','shard'}, use_global_device_ids=true, to_apply=%region_33.34 | all-reduce | flops 6144 | bytes 49152 | tf_op jit(solution)/shard_map/psum | solution.py:262
  696.0 59.8 %all-reduce.5.cloned.1.call-done = (f32[512,1536]{1,0:T(8,128)}, f32[512,512]{1,0:T(8,128)}) async-done(((f32[512,1536]{1,0:T(8,128)}, f32[512,512]{1,0:T(8,128)}), (f32[512,1536]{1,0:T(8,128)}, f32[512,512]{1,0:T(8,128)})) %all-reduce.5.cloned.1.call-update) | async-done | bytes 4194320 | tf_op jit(solution)/shard_map/psum | solution.py:262
  (262 shorter events, 197.3 us)
Async XLA Ops:
  7.2 17.6 %copy-start.8 = (bf16[788,512]{1,0:T(8,128)(2,1)S(1)}, bf16[788,512]{1,0:T(8,128)(2,1)}, u32[]{:S(2)}) copy-start(bf16[788,512]{1,0:T(8,128)(2,1)} %param.13) | copy-start | bytes 2420740
  7.2 18.2 %copy-start.32 = (bf16[128,512]{1,0:T(8,128)(2,1)S(1)}, bf16[128,512]{1,0:T(8,128)(2,1)}, u32[]{:S(2)}) copy-start(bf16[128,512]{1,0:T(8,128)(2,1)} %param.18) | copy-start | bytes 393220
  7.2 27.5 %all-gather.4.cloned.1.call-start = ((), (), s32[]{:S(2)}) async-start(), calls=%async_computation.8 | async-start | bytes 1966080 | tf_op jit(solution)/shard_map/all_gather | solution.py:63
  25.0 12.7 %copy-start.36 = (f32[788]{0:T(1024)}, f32[788]{0:T(1024)S(1)}, u32[]{:S(2)}) copy-start(f32[788]{0:T(1024)S(1)} %broadcast_multiply_fusion.2) | copy-start | bytes 9460
  34.6 30.5 %copy-start.48 = (f32[1,512]{1,0:T(1,128)}, f32[1,512]{1,0:T(1,128)S(1)}, u32[]{:S(2)}) copy-start(f32[1,512]{1,0:T(1,128)S(1)} %get-tuple-element.85) | copy-start | bytes 6148
  65.6 210.0 %copy-start.13 = (bf16[788,512]{1,0:T(8,128)(2,1)}, bf16[788,512]{1,0:T(8,128)(2,1)S(1)}, u32[]{:S(2)}) copy-start(bf16[788,512]{1,0:T(8,128)(2,1)S(1)} %add_convert_fusion) | copy-start | bytes 2420740
  85.0 12.3 %copy-start.56 = (bf16[1,128]{1,0:T(2,128)(2,1)S(1)}, bf16[1,128]{1,0:T(2,128)(2,1)}, u32[]{:S(2)}) copy-start(bf16[1,128]{1,0:T(2,128)(2,1)} %param.25) | copy-start | bytes 772
  85.0 79.8 %all-to-all-start = ((bf16[8,1,394,512]{3,2,1,0:T(8,128)(2,1)}), bf16[8,1,394,512]{3,2,1,0:T(8,128)(2,1)}, u32[]{:S(2)}, u32[]{:S(2)}) async-start(bf16[8,1,394,512]{3,2,1,0:T(8,128)(2,1)} %bitcast.10), calls=%async_computation | async-start | bytes 6553600 | tf_op jit(solution)/shard_map/all_to_all | solution.py:135
  90.7 25.5 %all-gather.6.cloned.1.call-start = ((), (), s32[]{:S(2)}) async-start(), calls=%async_computation.9 | async-start | bytes 2621440 | tf_op jit(solution)/shard_map/all_gather | solution.py:68
  91.4 87.7 %all-gather.8.cloned.1.call-start = ((), (), s32[]{:S(2)}) async-start(), calls=%async_computation.10 | async-start | bytes 2621440 | tf_op jit(solution)/shard_map/all_gather | solution.py:70
  196.1 74.4 %copy-start.53 = (bf16[128,8]{0,1:T(8,128)(2,1)S(1)}, bf16[128,8]{0,1:T(8,128)(2,1)}, u32[]{:S(2)}) copy-start(bf16[128,8]{0,1:T(8,128)(2,1)} %param.19) | copy-start | bytes 6148
  196.1 80.0 %copy-start.33 = (s32[788,2]{0,1:T(2,128)S(1)}, s32[788,2]{0,1:T(2,128)}, u32[]{:S(2)}) copy-start(s32[788,2]{0,1:T(2,128)} %param.16) | copy-start | bytes 18916
  196.1 81.0 %all-to-all-start.1 = ((bf16[8,1,394,512]{3,2,1,0:T(8,128)(2,1)}), bf16[8,1,394,512]{3,2,1,0:T(8,128)(2,1)}, u32[]{:S(2)}, u32[]{:S(2)}) async-start(bf16[8,1,394,512]{3,2,1,0:T(8,128)(2,1)} %fusion.21), calls=%async_computation.1 | async-start | bytes 6553600 | tf_op jit(solution)/shard_map/all_to_all | solution.py:138
  289.5 17.7 %copy-start.2 = (f32[788,512]{1,0:T(8,128)S(1)}, f32[788,512]{1,0:T(8,128)}, u32[]{:S(2)}) copy-start(f32[788,512]{1,0:T(8,128)} %copy-done.1) | copy-start | bytes 4841476
  289.5 17.7 %copy-start.28 = (bf16[788,512]{1,0:T(8,128)(2,1)S(1)}, bf16[788,512]{1,0:T(8,128)(2,1)}, u32[]{:S(2)}) copy-start(bf16[788,512]{1,0:T(8,128)(2,1)} %param.14) | copy-start | bytes 2420740
  339.6 91.0 %copy-start.58 = (bf16[1,2048,512]{2,1,0:T(8,128)(2,1)S(1)}, bf16[1,2048,512]{2,1,0:T(8,128)(2,1)}, u32[]{:S(2)}) copy-start(bf16[1,2048,512]{2,1,0:T(8,128)(2,1)} %all-gather.8.cloned.1.call-done) | copy-start | bytes 6291460
  430.6 25.7 %copy-start.12 = (bf16[8,1,394,512]{3,2,1,0:T(8,128)(2,1)}, bf16[8,1,394,512]{3,2,1,0:T(8,128)(2,1)S(1)}, u32[]{:S(2)}) copy-start(bf16[8,1,394,512]{3,2,1,0:T(8,128)(2,1)S(1)} %all_to_all.20) | copy-start | bytes 9682948
  430.6 30.4 %copy-start.57 = (bf16[1,512,2048]{2,1,0:T(8,128)(2,1)S(1)}, bf16[1,512,2048]{2,1,0:T(8,128)(2,1)}, u32[]{:S(2)}) copy-start(bf16[1,512,2048]{2,1,0:T(8,128)(2,1)} %all-gather.6.cloned.1.call-done) | copy-start | bytes 6291460
  469.8 77.2 %all-to-all-start.3 = ((bf16[8,1,394,512]{3,2,1,0:T(8,128)(2,1)}), bf16[8,1,394,512]{3,2,1,0:T(8,128)(2,1)}, u32[]{:S(2)}, u32[]{:S(2)}) async-start(bf16[8,1,394,512]{3,2,1,0:T(8,128)(2,1)} %convert_bitcast_fusion), calls=%async_computation.3 | async-start | bytes 6553600 | tf_op jit(solution)/shard_map/all_to_all | solution.py:207
  474.2 43.3 %reduce-scatter.15.cloned.1.call-start = ((), (), s32[]{:S(2)}) async-start(), calls=%async_computation.14 | async-start | bytes 163840
  477.8 44.9 %reduce-scatter.13.cloned.1.call-start = ((), (), s32[]{:S(2)}) async-start(), calls=%async_computation.13 | async-start | bytes 655360
  479.0 137.1 %reduce-scatter.11.cloned.1.call-start = ((), (), s32[]{:S(2)}) async-start(), calls=%async_computation.12 | async-start | bytes 2621440 | tf_op jit(solution)/shard_map/reduce_scatter | solution.py:279
  497.3 127.6 %reduce-scatter.9.cloned.1.call-start = ((), (), s32[]{:S(2)}) async-start(), calls=%async_computation.11 | async-start | bytes 2621440 | tf_op jit(solution)/shard_map/reduce_scatter | solution.py:273
  517.1 238.7 %all-reduce.5.cloned.1.call-start = ((), (), s32[]{:S(2)}) async-start(), calls=%async_computation.15 | async-start | bytes 8388608 | tf_op jit(solution)/shard_map/psum | solution.py:262
  (49 other events, 180.9 us)
Sparse Core Ops, SparseCore 0:
  9.6 23.7 all-gather.3
  93.1 23.0 all-gather.5
  117.7 22.5 all-gather.7
  477.9 19.9 reduce-scatter.14
  500.9 21.6 reduce-scatter.12
  525.0 31.4 reduce-scatter.10
  559.1 31.3 reduce-scatter.8
  614.9 140.7 all-reduce.4
